TPU v7x, 32 devices: a whole 2x2x4 slice. The times are simulated.
32 devices in a mesh: group: 2 (over x), vocab: 16 (over z, y, core).
Axes of the slice: x: 2, y: 2, z: 4, core: 2. Of those that a mesh axis runs over, the one named last changes fastest.
Arguments:
- table: bfloat16 [4608, 12288], P('vocab', 'group')
- hidden: bfloat16 [448, 4608], P(None, 'vocab')
- gain: bfloat16 [4608], P('vocab'), may hold values from 0.099609375 to 1.8984375
- ids: int32 [448], replicated, may hold values from 0 to 12287
Outputs:
- next_embed: bfloat16 [448, 4608], P(None, 'vocab')
- logprobs: float32 [448, 12288], P(None, ('group', 'vocab'))
- chosen: float32 [448], replicated
All inputs are finite; a program needn't handle non-finite values.
Results may differ from a plain program's by a relative error of at most 0.001.
Values may be sent and summed in bfloat16 or wider, within the bound.
A program may use at most 64 MiB of HBM per device.

v0:
```python
import math

import jax
import jax.numpy as jnp
from jax import lax
from jax.sharding import PartitionSpec as P


def body(table, hidden, gain, ids):
    share, span_cols = table.shape
    groups_n = lax.axis_size("vocab")
    voc_cols = span_cols // groups_n
    width = share * groups_n
    group_index = lax.axis_index("group")
    vocab_index = lax.axis_index("vocab")
    local_ids = ids - group_index * span_cols
    inside = jnp.logical_and(local_ids >= 0, local_ids < span_cols)
    found = jnp.take(table, jnp.clip(local_ids, 0, span_cols - 1), axis=1).astype(jnp.float32).T
    found = found * inside[:, None].astype(jnp.float32)
    embed_cols = lax.psum(found.astype(jnp.bfloat16), "group").astype(jnp.float32)
    next_embed = (embed_cols * math.sqrt(width)).astype(jnp.bfloat16)
    states = hidden.astype(jnp.float32)
    part_sq = jnp.sum(states * states, axis=1)
    total_sq = lax.psum(part_sq, "vocab")
    scale_row = lax.rsqrt(total_sq / width + 1e-06)
    normed_share = (states * gain.astype(jnp.float32) * scale_row[:, None]).astype(jnp.bfloat16)
    normed = lax.all_gather(normed_share, "vocab", axis=1, tiled=True)
    full_cols = lax.all_to_all(table, "vocab", split_axis=1, concat_axis=0, tiled=True)
    logits = jnp.dot(normed, full_cols, preferred_element_type=jnp.float32)
    capped = 30.0 * jnp.tanh(logits / 30.0)
    first_col = (group_index * groups_n + vocab_index) * voc_cols
    offsets = ids - first_col
    columns = lax.broadcasted_iota(jnp.int32, capped.shape, 1)
    pick = jnp.sum(jnp.where(columns == offsets[:, None], capped, 0.0), axis=1)
    sums, picks = lax.psum((jnp.sum(jnp.exp(capped), axis=1), pick), ("group", "vocab"))
    log_total = jnp.log(sums)
    logprobs = capped - log_total[:, None]
    chosen = picks - log_total
    return (next_embed, logprobs, chosen)


def solution(mesh):
    placed = (P("vocab", "group"), P(None, "vocab"), P("vocab"), P())
    return jax.shard_map(
        body,
        mesh=mesh,
        in_specs=placed,
        out_specs=(P(None, "vocab"), P(None, ("group", "vocab")), P()),
        check_vma=False,
    )
```

profile of v0, /device:TPU:0, one launch (start us, length us, event | category | flops | bytes accessed | tf_op | source)
XLA Modules:
  0.0 228.5 jit_solution(8702829267844787670)
XLA Ops:
  8.0 0.0 all-reduce.3.cloned.1.call-start
  8.0 0.7 compare_and_fusion
  8.8 0.0 copy-start.2
  8.8 0.0 copy-start
  8.8 6.4 %copy.14 = bf16[288,6144]{0,1:T(8,128)(2,1)} copy(bf16[288,6144]{1,0:T(8,128)(2,1)} %param.4) | data formatting | bytes 7077888 | tf_op args[0]
  15.2 5.4 %gather_fusion = bf16[448,288]{1,0:T(8,128)(2,1)} fusion(bf16[288,6144]{0,1:T(8,128)(2,1)} %copy.14, s32[1024]{0:T(1024)S(1)} %pad_clamp_fusion), kind=kCustom, calls=%fused_computation | custom fusion | bytes 517888 | tf_op jit(solution)/shard_map/jit(_take)/gather | solution.py:18
  20.6 1.9 multiply_convert_fusion
  22.5 0.0 all-reduce.3.cloned.1.call-update
  22.5 0.0 all-gather.2.cloned.1.call-start
  22.5 1.1 fusion.4
  23.6 34.9 %psum.29 = f32[448]{0:T(512)S(1)} all-reduce(f32[448]{0:T(512)S(1)} %fusion.4), channel_id=1, replica_groups=mesh['group'=2,'vocab'=16] {'vocab'}, use_global_device_ids=true, to_apply=%region_2.3 | all-reduce | flops 448 | bytes 3584 | tf_op jit(solution)/shard_map/psum | solution.py:24
  58.5 0.0 copy-done.2
  58.6 1.8 fusion.3
  60.4 0.0 all-gather.2.cloned.1.call-update
  60.4 0.0 copy-done
  60.4 2.1 copy.19
  62.5 0.0 copy-start.1
  62.5 3.9 %all-to-all-start = ((bf16[288,16,384]{2,0,1:T(8,128)(2,1)}), bf16[288,16,384]{2,0,1:T(8,128)(2,1)S(1)}, u32[]{:S(2)}, u32[]{:S(2)}) async-start(bf16[288,16,384]{2,0,1:T(8,128)(2,1)} %bitcast.8), calls=%async_computation | async-start | bytes 7077888 | tf_op jit(solution)/shard_map/all_to_all | solution.py:28
  66.5 0.0 copy-done.1
  66.5 0.0 all-reduce.3.cloned.1.call-done
  66.5 1.8 multiply_convert_fusion.1
  68.3 1.8 copy.16
  70.1 90.3 %all-to-all-done = bf16[288,16,384]{2,0,1:T(8,128)(2,1)S(1)} async-done(((bf16[288,16,384]{2,0,1:T(8,128)(2,1)}), bf16[288,16,384]{2,0,1:T(8,128)(2,1)S(1)}, u32[]{:S(2)}, u32[]{:S(2)}) %all-to-all-start) | async-done | bytes 3538976 | tf_op jit(solution)/shard_map/all_to_all | solution.py:28
  160.4 0.0 all-gather.2.cloned.1.call-done
  160.4 5.6 %select_reduce_fusion = (f32[448]{0:T(512)S(1)}, f32[448]{0:T(512)S(1)}, f32[448,384]{1,0:T(8,128)}) fusion(s32[448]{0:T(512)S(1)} %broadcast_subtract_fusion.1, bf16[448,4608]{0,1:T(8,128)(2,1)} %all-gather.2.cloned.1.call-done, bf16[4608,384]{1,0:T(8,128)(2,1)S(1)} %bitcast.10), kind=kOutput, calls=%fused_computation.8 | convolution fusion | flops 1586478080 | bytes 8361216 | tf_op jit(solution)/shard_map/dot_general | solution.py:29
  166.0 52.4 %all-reduce = (f32[448]{0:T(512)S(1)}, f32[448]{0:T(512)S(1)}) all-reduce(f32[448]{0:T(512)S(1)} %get-tuple-element.16, f32[448]{0:T(512)S(1)} %get-tuple-element.15), channel_id=1, replica_groups=mesh['group'=2,'vocab'=16] {'group','vocab'}, use_global_device_ids=true, to_apply=%region_4.5 | all-reduce | flops 896 | bytes 7168 | tf_op jit(solution)/shard_map/psum | solution.py:35
  218.4 0.6 log_subtract_fusion
  219.0 2.1 broadcast_subtract_fusion
  (4 shorter events, 0.0 us)
Async XLA Ops:
  8.0 58.5 %all-reduce.3.cloned.1.call-start = ((), (), s32[]{:S(2)}) async-start(), calls=%async_computation.1 | async-start | bytes 688128 | tf_op jit(solution)/shard_map/psum | solution.py:20
  8.8 49.8 %copy-start.2 = (bf16[288]{0:T(512)(128)(2,1)S(1)}, bf16[288]{0:T(512)(128)(2,1)}, u32[]{:S(2)}) copy-start(bf16[288]{0:T(512)(128)(2,1)} %param.6) | copy-start | bytes 1732
  8.8 51.7 %copy-start = (bf16[288,6144]{1,0:T(8,128)(2,1)S(1)}, bf16[288,6144]{1,0:T(8,128)(2,1)}, u32[]{:S(2)}) copy-start(bf16[288,6144]{1,0:T(8,128)(2,1)} %param.4) | copy-start | bytes 10616836
  22.5 137.9 %all-gather.2.cloned.1.call-start = ((), (), s32[]{:S(2)}) async-start(), calls=%async_computation.2 | async-start | bytes 5013504 | tf_op jit(solution)/shard_map/all_gather | solution.py:27
  62.5 3.9 %copy-start.1 = (s32[448]{0:T(512)S(1)}, s32[448]{0:T(512)}, u32[]{:S(2)}) copy-start(s32[448]{0:T(512)} %param.7) | copy-start | bytes 5380
  62.5 97.9 %all-to-all-start = ((bf16[288,16,384]{2,0,1:T(8,128)(2,1)}), bf16[288,16,384]{2,0,1:T(8,128)(2,1)S(1)}, u32[]{:S(2)}, u32[]{:S(2)}) async-start(bf16[288,16,384]{2,0,1:T(8,128)(2,1)} %bitcast.8), calls=%async_computation | async-start | bytes 7077888 | tf_op jit(solution)/shard_map/all_to_all | solution.py:28
Sparse Core Ops, SparseCore 0:
  22.6 27.4 all-reduce.2
Sparse Core Ops, SparseCore 1:
  60.5 97.0 all-gather.1
where the time goes:
time: 229 us
  waiting for transfers between devices  90.4 us (39%)
  blocking collectives  87.4 us (38%)
  local copies, waits for them, and re-layouts  15.8 us (7%)
  between operations  15.6 us (7%)
  other arithmetic  9.93 us (4%)
  matrix products  5.62 us (2%)
  starting transfers between devices  3.98 us (2%)
    all_to_all x1, waiting for transfers between devices, body(): lax.all_to_all(table, 'vocab', split_axis=1, concat_axis=0, tiled=True)  90.3 us
    psum x1, blocking collectives, body(): lax.psum((jnp.sum(jnp.exp(capped), axis=1), pick), ('group', 'vocab'))  52.4 us
    psum x1, blocking collectives, body(): total_sq = lax.psum(part_sq, 'vocab')  34.9 us
    unnamed x8, local copies, waits for them, and re-layouts  8.27 us
    dot_general x1, matrix products, body(): logits = jnp.dot(normed, full_cols, preferred_element_type=jnp.float32)  5.62 us
    gather x1, local copies, waits for them, and re-layouts, body(): jnp.take(table, jnp.clip(local_ids, 0, span_cols - 1), axis=1)  5.37 us
  transfers between devices with their start and end apart: 3, of which 1 were waited for; matrix products, arithmetic and copies ran while one was open for 4% of the time, Pallas kernels for 0%

commit v1 on v0

v1 whole, which is shorter than its diff:
```python
import functools
import math

import jax
import jax.numpy as jnp
from jax import lax
from jax.experimental import pallas as pl
from jax.experimental.pallas import tpu as pltpu
from jax.sharding import PartitionSpec as P

MESH = pl.DeviceIdType.MESH
NT = (((1,), (1,)), ((), ()))
HIGH = lax.Precision.HIGHEST


def peers_order(nz):
    ks = sorted(range(1, nz), key=lambda k: -min(k, nz - k))
    return ks + [0]


def kernel(
    sizes, table, hidden, gain, ids, embed_out, capped_out, stats_out,
    tab_v, tpar, hpar, gpar, own_n, par_n, ysend, yrecv, zsend, zrecv, acc,
    xsend, xrecv, found, msend, mrecv, ssend, srecv, local_sem, send_sem, recv_sem,
):
    groups, share, width, n_tok, span, voc_cols, nz = sizes
    g = lax.axis_index("group")
    v = lax.axis_index("vocab")
    c, y, z = lax.rem(v, 2), lax.rem(v // 2, 2), v // 4
    core_peer = (g, v + 1 - 2 * c)
    y_peer = (g, v + 2 - 4 * y)

    def z_peer(k):
        return (g, lax.rem(z + k, nz) * 4 + y * 2 + c)

    def g_peer(d):
        return (lax.rem(g + d, groups), v)

    def column(zz, yy, cc):
        return pl.ds(pl.multiple_of((zz * 4 + yy * 2 + cc) * voc_cols, 128), voc_cols)

    order = peers_order(nz)
    started = []

    def send(src, dst, peer):
        i = len(started)
        copy = pltpu.make_async_remote_copy(
            src_ref=src, dst_ref=dst, send_sem=send_sem.at[i], recv_sem=recv_sem.at[i],
            device_id=peer, device_id_type=MESH,
        )
        copy.start()
        started.append(copy)
        return copy

    load = pltpu.make_async_copy(table, tab_v, local_sem)
    load.start()

    barrier = pltpu.get_barrier_semaphore()
    everyone = [core_peer, y_peer]
    everyone += [z_peer(k) for k in range(1, nz)]
    everyone += [g_peer(d) for d in range(1, groups)]
    for peer in everyone:
        pl.semaphore_signal(barrier, inc=1, device_id=peer, device_id_type=MESH)

    states = hidden[...].astype(jnp.float32)
    ones = jnp.ones((8, share), jnp.float32)
    sq = lax.dot_general(ones, states * states, NT, precision=HIGH,
                         preferred_element_type=jnp.float32)
    msend[0] = sq
    pl.semaphore_wait(barrier, len(everyone))

    first_ms = send(msend.at[0], mrecv.at[0], core_peer)
    h_copy = send(hidden, hpar, core_peer)
    g_copy = send(gain, gpar, core_peer)
    t_copies = []
    for i, k in enumerate(order):
        zz = lax.rem(z + k, nz)
        for half, yy in enumerate((1 - y, y)):
            t_copies.append(send(table.at[:, column(zz, yy, 1 - c)], tpar.at[2 * i + half], core_peer))

    first_ms.wait_recv()
    sq = sq + mrecv[0]
    msend[1] = sq
    send(msend.at[1], mrecv.at[1], y_peer).wait_recv()
    sq = sq + mrecv[1]
    msend[2] = sq
    copies = [send(msend.at[2], mrecv.at[1 + k], z_peer(k)) for k in range(1, nz)]
    for k, copy in enumerate(copies):
        copy.wait_recv()
        sq = sq + mrecv[2 + k]
    scale = lax.rsqrt(sq / width + 1e-06).T[:, :1]

    own_n[...] = (states * gain[...] * scale).astype(jnp.bfloat16)
    h_copy.wait_recv()
    g_copy.wait_recv()
    par_n[...] = (hpar[...].astype(jnp.float32) * gpar[...] * scale).astype(jnp.bfloat16)
    load.wait()

    def partial(i, half, zz, yy):
        t_copies[2 * i + half].wait_recv()
        first = jnp.dot(own_n[...], tab_v[:, column(zz, yy, c)], preferred_element_type=jnp.float32)
        return first + jnp.dot(par_n[...], tpar[2 * i + half], preferred_element_type=jnp.float32)

    y_copies = []
    for i, k in enumerate(order):
        zz = lax.rem(z + k, nz)
        ysend[i] = partial(i, 0, zz, 1 - y).astype(jnp.bfloat16)
        y_copies.append(send(ysend.at[i], yrecv.at[i], y_peer))

    chunk = 2 * voc_cols
    inside = ids[...] - g * span
    found[...] = jnp.zeros_like(found)

    def gather(n, carry):
        start = n * chunk
        places = lax.broadcasted_iota(jnp.int32, (n_tok, chunk), 1)
        hot = jnp.where(places == inside - start, 1.0, 0.0).astype(jnp.bfloat16)
        found[...] += lax.dot_general(
            hot, tab_v[:, pl.ds(pl.multiple_of(start, 128), chunk)], NT,
            preferred_element_type=jnp.float32)
        return carry

    lax.fori_loop(0, span // chunk, gather, 0)
    xsend[...] = found[...].astype(jnp.bfloat16)
    x_copies = [send(xsend, xrecv.at[d - 1], g_peer(d)) for d in range(1, groups)]

    z_copies = {}
    for i, k in enumerate(order):
        zz = lax.rem(z + k, nz)
        both = partial(i, 1, zz, y)
        y_copies[i].wait_recv()
        both = both + yrecv[i].astype(jnp.float32)
        if k:
            zsend[k - 1] = both.astype(jnp.bfloat16)
            z_copies[k] = send(zsend.at[k - 1], zrecv.at[k - 1], z_peer(k))
        else:
            acc[...] = both

    embed = found[...]
    for d, copy in enumerate(x_copies):
        copy.wait_recv()
        embed = embed + xrecv[d].astype(jnp.float32)
    embed_out[...] = embed.astype(jnp.bfloat16)

    logits = acc[...]
    for k in order[:-1]:
        z_copies[k].wait_recv()
        logits = logits + zrecv[k - 1].astype(jnp.float32)
    capped = 30.0 * jnp.tanh(logits / 30.0)
    capped_out[...] = capped
    first_col = (g * 4 * nz + v) * voc_cols
    places = lax.broadcasted_iota(jnp.int32, (n_tok, voc_cols), 1)
    pick = jnp.where(places == ids[...] - first_col, capped, 0.0)
    ones = jnp.ones((8, voc_cols), jnp.float32)
    sums = lax.dot_general(ones, jnp.exp(capped), NT, precision=HIGH,
                           preferred_element_type=jnp.float32)
    picks = lax.dot_general(ones, pick, NT, precision=HIGH,
                            preferred_element_type=jnp.float32)
    slot = 0
    stages = [[core_peer], [y_peer], [z_peer(k) for k in range(1, nz)],
              [g_peer(d) for d in range(1, groups)]]
    for stage, peers in enumerate(stages):
        ssend[stage, 0] = sums
        ssend[stage, 1] = picks
        copies = []
        for peer in peers:
            copies.append((slot, send(ssend.at[stage], srecv.at[slot], peer)))
            slot += 1
        for at, copy in copies:
            copy.wait_recv()
            sums = sums + srecv[at, 0]
            picks = picks + srecv[at, 1]
    stats_out[0] = sums
    stats_out[1] = picks
    for copy in started:
        copy.wait_send()


def body(table, hidden, gain, ids):
    share, span = table.shape
    n_tok = hidden.shape[0]
    vocab_n = lax.axis_size("vocab")
    groups = lax.axis_size("group")
    voc_cols = span // vocab_n
    width = share * vocab_n
    nz = vocab_n // 4
    half = vocab_n // 2
    peers = 2 + (nz - 1) + (groups - 1)
    n_copies = (nz + 1) + 2 + half + nz + (groups - 1) + (nz - 1) + peers
    bf16, f32 = jnp.bfloat16, jnp.float32
    sizes = (groups, share, width, n_tok, span, voc_cols, nz)
    vmem = pl.BlockSpec(memory_space=pltpu.VMEM)
    found, capped, stats = pl.pallas_call(
        functools.partial(kernel, sizes),
        out_shape=(
            jax.ShapeDtypeStruct((n_tok, share), bf16),
            jax.ShapeDtypeStruct((n_tok, voc_cols), f32),
            jax.ShapeDtypeStruct((2, 8, n_tok), f32),
        ),
        in_specs=[pl.BlockSpec(memory_space=pl.ANY), vmem, vmem, vmem],
        out_specs=(vmem, vmem, vmem),
        scratch_shapes=[
            pltpu.VMEM((share, span), bf16),
            pltpu.VMEM((half, share, voc_cols), bf16),
            pltpu.VMEM((n_tok, share), bf16),
            pltpu.VMEM((1, share), f32),
            pltpu.VMEM((n_tok, share), bf16),
            pltpu.VMEM((n_tok, share), bf16),
            pltpu.VMEM((nz, n_tok, voc_cols), bf16),
            pltpu.VMEM((nz, n_tok, voc_cols), bf16),
            pltpu.VMEM((nz - 1, n_tok, voc_cols), bf16),
            pltpu.VMEM((nz - 1, n_tok, voc_cols), bf16),
            pltpu.VMEM((n_tok, voc_cols), f32),
            pltpu.VMEM((n_tok, share), bf16),
            pltpu.VMEM((groups - 1, n_tok, share), bf16),
            pltpu.VMEM((n_tok, share), f32),
            pltpu.VMEM((3, 8, n_tok), f32),
            pltpu.VMEM((nz + 1, 8, n_tok), f32),
            pltpu.VMEM((4, 2, 8, n_tok), f32),
            pltpu.VMEM((peers, 2, 8, n_tok), f32),
            pltpu.SemaphoreType.DMA,
            pltpu.SemaphoreType.DMA((n_copies,)),
            pltpu.SemaphoreType.DMA((n_copies,)),
        ],
        compiler_params=pltpu.CompilerParams(
            collective_id=0, has_side_effects=True, vmem_limit_bytes=60 * 1024 * 1024
        ),
    )(table, hidden, gain.astype(f32)[None, :], ids[:, None])
    next_embed = (found.astype(f32) * math.sqrt(width)).astype(bf16)
    log_total = jnp.log(stats[0, 0])
    logprobs = capped - log_total[:, None]
    chosen = stats[1, 0] - log_total
    return (next_embed, logprobs, chosen)


def solution(mesh):
    placed = (P("vocab", "group"), P(None, "vocab"), P("vocab"), P())
    return jax.shard_map(
        body,
        mesh=mesh,
        in_specs=placed,
        out_specs=(P(None, "vocab"), P(None, ("group", "vocab")), P()),
        check_vma=False,
    )
```

time: 229 us -> 77.3 us (0.34)
  waiting for transfers between devices: 90.4 us -> 0 us
  blocking collectives: 87.4 us -> 0 us
  Pallas kernels: 0 us -> 66.4 us
  between operations: 15.6 us -> 0.64 us
  local copies, waits for them, and re-layouts: 15.8 us -> 6.25 us
  other arithmetic: 9.93 us -> 3.7 us
  matrix products: 5.62 us -> 0 us
  starting transfers between devices: 3.98 us -> 0 us
    all_to_all x1 -> x0, waiting for transfers between devices: 90.3 us -> none  [body(): lax.all_to_all(table, 'vocab', split_axis=1, concat_axis=0, tiled=True)]
    psum x2 -> x0, blocking collectives: 87.4 us -> none  [the longest x1 52.4 us: body(): lax.psum((jnp.sum(jnp.exp(capped), axis=1), pick), ('group', 'vocab'))]
    pallas_call x0 -> x1, Pallas kernels: none -> 66.4 us  [body(): pl.pallas_call(functools.partial(kernel, sizes), out_shape=(jax.ShapeDtyp...]
    dot_general x1 -> x0, matrix products: 5.62 us -> none  [body(): logits = jnp.dot(normed, full_cols, preferred_element_type=jnp.float32)]
    unnamed x8 -> x2, local copies, waits for them, and re-layouts: 8.27 us -> 2.76 us
    gather x1 -> x0, local copies, waits for them, and re-layouts: 5.37 us -> none  [body(): jnp.take(table, jnp.clip(local_ids, 0, span_cols - 1), axis=1)]
    convert_element_type x4 -> x1, other arithmetic: 5.51 us -> 1.05 us  [body(): next_embed = (found.astype(f32) * math.sqrt(width)).astype(bf16)]
    all_to_all x1 -> x0, starting transfers between devices: 3.9 us -> none  [body(): lax.all_to_all(table, 'vocab', split_axis=1, concat_axis=0, tiled=True)]
  transfers between devices with their start and end apart: 3 -> 0, of which waited for: 1 -> 0; matrix products, arithmetic and copies ran while one was open for 4% -> 0% of each run, Pallas kernels for 0% -> 0%
where the time goes in v1:
time: 77.3 us; the launch traced here: 77 us
  Pallas kernels  66.4 us (86%)
  local copies, waits for them, and re-layouts  6.25 us (8%)
  other arithmetic  3.7 us (5%)
    pallas_call x1, Pallas kernels, body(): pl.pallas_call(functools.partial(kernel, sizes), out_shape=(jax.ShapeDtyp...  66.4 us
    unnamed x2, local copies, waits for them, and re-layouts  2.76 us
    sub x1, other arithmetic, body(): logprobs = capped - log_total[:, None]  2.08 us

profile of v1, /device:TPU:0, one launch (start us, length us, event | category | flops | bytes accessed | tf_op | source)
XLA Modules:
  0.0 77.0 jit_solution(10724399669107060919)
XLA Ops:
  0.6 1.2 %reshape.12.gain = f32[1,288]{1,0:T(1,128)} reshape(bf16[288]{0:T(512)(128)(2,1)} %param.6) | data formatting | bytes 1728 | tf_op jit(solution)/shard_map/broadcast_in_dim | solution.py:228
  1.9 1.5 %copy.10.ids = s32[448,1]{1,0:T(8,128)} copy(s32[448,1]{0,1:T(1,128)} %bitcast.6) | data formatting | bytes 3584 | tf_op jit(solution)/shard_map/broadcast_in_dim | solution.py:228
  3.4 1.9 %copy.9.hidden = bf16[448,288]{1,0:T(8,128)(2,1)} copy(bf16[448,288]{0,1:T(8,128)(2,1)} %param.5) | data formatting | bytes 516096 | tf_op args[1]
  5.3 66.4 %shard_map.67 = (bf16[448,288]{1,0:T(8,128)(2,1)}, f32[448,384]{1,0:T(8,128)}, f32[2,8,448]{2,1,0:T(8,128)}) custom-call(bf16[288,6144]{1,0:T(8,128)(2,1)} %table.1, bf16[448,288]{1,0:T(8,128)(2,1)} %copy.9.hidden, f32[1,288]{1,0:T(1,128)} %reshape.12.gain, s32[448,1]{1,0:T(8,128)} %copy.10.ids), custom_call_target="tpu_custom_call" | custom-call | tf_op jit(solution)/shard_map/pallas_call | solution.py:193
  71.6 1.0 %multiply_convert_fusion = bf16[448,288]{1,0:T(8,128)(2,1)S(1)} fusion(bf16[448,288]{1,0:T(8,128)(2,1)} %get-tuple-element.6), kind=kLoop, calls=%fused_computation | loop fusion | flops 387072 | bytes 516096 | tf_op jit(solution)/shard_map/convert_element_type | solution.py:229
  72.7 0.9 %copy.11 = bf16[448,288]{0,1:T(8,128)(2,1)} copy(bf16[448,288]{1,0:T(8,128)(2,1)S(1)} %multiply_convert_fusion) | data formatting | bytes 516096
  73.6 0.7 fusion
  74.3 2.1 %broadcast_subtract_fusion = f32[448,384]{1,0:T(8,128)} fusion(f32[448,384]{1,0:T(8,128)} %get-tuple-element.7, f32[448]{0:T(512)S(1)} %bitcast.3), kind=kLoop, calls=%fused_computation.1 | loop fusion | flops 172032 | bytes 1378048 | tf_op jit(solution)/shard_map/sub | solution.py:231
  76.4 0.6 sub.13

commit v2 on v0

v2 whole, which is shorter than its diff:
```python
import functools
import math

import jax
import jax.numpy as jnp
from jax import lax
from jax.experimental import pallas as pl
from jax.experimental.pallas import tpu as pltpu
from jax.sharding import PartitionSpec as P

MESH = pl.DeviceIdType.MESH


def stage_bits(half, bits):
    dims = list(range(bits))
    if half == 0:
        dims[0], dims[1] = dims[1], dims[0]
    return [1 << d for d in dims]


def stage_of(half, mask, bits):
    for stage, bit in enumerate(stage_bits(half, bits)):
        if mask & bit:
            return stage
    return bits


def program_order(bits):
    if bits == 3:
        return [(1, 7), (0, 7), (0, 6), (1, 5), (0, 3), (0, 2), (0, 5), (1, 3), (0, 1), (1, 1),
                None, (1, 6), (1, 4), (0, 4), (1, 2)]
    every = [(half, mask) for mask in range((1 << bits) - 1, 0, -1) for half in (1, 0)]
    every.sort(key=lambda one: stage_of(one[0], one[1], bits))
    return every + [None]


def kernel(
    sizes, table, hidden, gain, ids, embed_out, capped_out, stats_out,
    tab_v, tpar, hown, hpar, gpar, own_n, par_n, send0, recv0, send1, recv1,
    xsend, xrecv, found, msend, mrecv, ssend, srecv, local_sem, send_sem, recv_sem,
):
    groups, share, width, n_tok, span, voc_cols, nz, bits, split = sizes
    f32, bf16 = jnp.float32, jnp.bfloat16
    g = lax.axis_index("group")
    v = lax.axis_index("vocab")
    c, y, z = v % 2, (v // 2) % 2, v // 4
    rows = ((0, split), (split, n_tok))
    sends, recvs = (send0, send1), (recv0, recv1)

    def flip(value, on):
        return 1 - value if on else value

    def place(mask, core):
        zz = 0
        for i in range(bits - 1):
            zz = zz + (1 << i) * flip((z // (1 << i)) % 2, (mask >> (i + 1)) & 1)
        return zz * 4 + flip(y, mask & 1) * 2 + core

    def z_peer(k):
        return (g, ((z + k) % nz) * 4 + y * 2 + c)

    def near_peer(d, m):
        gg = (g + d) % groups if d else g
        return (gg, z * 4 + flip(y, m & 1) * 2 + flip(c, m & 2))

    core_peer = near_peer(0, 2)
    z_peers = [z_peer(k) for k in range(1, nz)]
    near_vocab = [near_peer(0, m) for m in range(1, 4)]
    near_all = near_vocab + [near_peer(d, m) for d in range(1, groups) for m in range(4)]

    def column(mask, core):
        return pl.ds(pl.multiple_of(place(mask, core) * voc_cols, 128), voc_cols)

    started = []

    def send(src, dst, peer):
        i = len(started)
        copy = pltpu.make_async_remote_copy(
            src_ref=src, dst_ref=dst, send_sem=send_sem.at[i], recv_sem=recv_sem.at[i],
            device_id=peer, device_id_type=MESH,
        )
        copy.start()
        started.append(copy)
        return copy

    h_load = pltpu.make_async_copy(hidden, hown, local_sem.at[0])
    h_load.start()
    load = pltpu.make_async_copy(table, tab_v, local_sem.at[1])
    load.start()

    barrier = pltpu.get_barrier_semaphore()
    everyone = z_peers + near_all
    for peer in everyone:
        pl.semaphore_signal(barrier, inc=1, device_id=peer, device_id_type=MESH)

    h_load.wait()
    states = hown[...].astype(f32)
    sq = jnp.broadcast_to(jnp.sum(states * states, axis=0, keepdims=True), (8, n_tok))
    msend[0] = sq
    own_t = states.T * gain[...].astype(f32).reshape(1, share)
    pl.semaphore_wait(barrier, len(everyone))

    copies = [send(msend.at[0], mrecv.at[j], peer) for j, peer in enumerate(z_peers)]
    h_copy = send(hidden, hpar, core_peer)
    g_copy = send(gain, gpar, core_peer)
    order = program_order(bits)
    uses = []
    for one in order:
        if one and one[1] not in uses:
            uses.append(one[1])
    t_copies = {}
    for mask in uses + [0]:
        t_copies[mask] = send(table.at[:, column(mask, 1 - c)], tpar.at[mask], core_peer)

    h_copy.wait_recv()
    g_copy.wait_recv()
    par_t = hpar[...].astype(f32).T * gpar[...].astype(f32).reshape(1, share)

    for j, copy in enumerate(copies):
        copy.wait_recv()
        sq = sq + mrecv[j]
    msend[1] = sq
    copies = [send(msend.at[1], mrecv.at[nz - 1 + j], peer) for j, peer in enumerate(near_vocab)]
    for j, copy in enumerate(copies):
        copy.wait_recv()
        sq = sq + mrecv[nz - 1 + j]
    scale = lax.rsqrt(sq / width + 1e-06).T[:, :1]
    own_n[...] = (own_t * scale).astype(bf16)
    par_n[...] = (par_t * scale).astype(bf16)
    load.wait()

    landed = set()

    def partial(half, mask):
        if mask not in landed:
            t_copies[mask].wait_recv()
            landed.add(mask)
        low, high = rows[half]
        first = jnp.dot(own_n[low:high], tab_v[:, column(mask, c)], preferred_element_type=f32)
        return first + jnp.dot(par_n[low:high], tpar[mask], preferred_element_type=f32)

    arrivals = {}

    def reduced(half, mask):
        total = partial(half, mask)
        for bit in stage_bits(half, bits)[:stage_of(half, mask, bits)]:
            arrivals[half, mask | bit].wait_recv()
            total = total + recvs[half][(mask | bit) - 1].astype(f32)
        return total

    chunk = 2 * voc_cols
    local_ids = ids[...].reshape(1, n_tok) - g * span

    def gather(n, carry):
        start = n * chunk
        spots = lax.broadcasted_iota(jnp.int32, (chunk, n_tok), 0)
        hot = jnp.where(spots == local_ids - start, 1.0, 0.0).astype(bf16)
        found[...] += jnp.dot(tab_v[:, pl.ds(pl.multiple_of(start, 128), chunk)], hot,
                              preferred_element_type=f32)
        return carry

    x_copies = []
    for one in order:
        if one is None:
            found[...] = jnp.zeros_like(found)
            lax.fori_loop(0, span // chunk, gather, 0)
            xsend[...] = found[...].astype(bf16)
            x_copies = [send(xsend, xrecv.at[d - 1], near_peer(d, 0)) for d in range(1, groups)]
            continue
        half, mask = one
        sends[half][mask - 1] = reduced(half, mask).astype(bf16)
        bit = stage_bits(half, bits)[stage_of(half, mask, bits)]
        peer = (g, place(bit, c))
        arrivals[half, mask] = send(sends[half].at[mask - 1], recvs[half].at[mask - 1], peer)

    embed = found[...]
    for d, copy in enumerate(x_copies):
        copy.wait_recv()
        embed = embed + xrecv[d].astype(f32)
    embed_out[...] = (embed * math.sqrt(width)).astype(bf16)

    first_col = (g * 4 * nz + v) * voc_cols
    offsets = jnp.broadcast_to(ids[...].reshape(1, n_tok), (8, n_tok)).astype(f32).T[:, :1].astype(jnp.int32)
    sums, picks = [], []
    for half, (low, high) in enumerate(rows):
        capped = 30.0 * jnp.tanh(reduced(half, 0) / 30.0)
        capped_out[low:high] = capped
        spots = lax.broadcasted_iota(jnp.int32, capped.shape, 1)
        pick = jnp.where(spots == offsets[low:high] - first_col, capped, 0.0)
        sums.append(jnp.sum(jnp.exp(capped), axis=1, keepdims=True))
        picks.append(jnp.sum(pick, axis=1, keepdims=True))
    sums = jnp.broadcast_to(jnp.concatenate(sums, axis=0), (n_tok, 8)).T
    picks = jnp.broadcast_to(jnp.concatenate(picks, axis=0), (n_tok, 8)).T
    slot = 0
    for phase, peers in enumerate((z_peers, near_all)):
        ssend[phase, 0] = sums
        ssend[phase, 1] = picks
        copies = []
        for peer in peers:
            copies.append((slot, send(ssend.at[phase], srecv.at[slot], peer)))
            slot += 1
        for at, copy in copies:
            copy.wait_recv()
            sums = sums + srecv[at, 0]
            picks = picks + srecv[at, 1]
    stats_out[0] = sums
    stats_out[1] = picks
    for copy in started:
        copy.wait_send()


def finish(embed, capped, stats, embed_out, logprobs_out, chosen_out):
    log_total = jnp.log(stats[0])
    embed_out[...] = embed[...]
    logprobs_out[...] = capped[...] - log_total.T[:, :1]
    chosen_out[...] = (stats[1] - log_total)[:1]


def body(table, hidden, gain, ids):
    share, span = table.shape
    n_tok = hidden.shape[0]
    vocab_n = lax.axis_size("vocab")
    groups = lax.axis_size("group")
    voc_cols = span // vocab_n
    width = share * vocab_n
    nz = vocab_n // 4
    half = vocab_n // 2
    bits = half.bit_length() - 1
    split = n_tok // 64 * 16
    near = 3 + 4 * (groups - 1)
    n_copies = (nz - 1) + 3 + 2 + half + 2 * (half - 1) + (groups - 1) + (nz - 1) + near
    bf16, f32 = jnp.bfloat16, jnp.float32
    sizes = (groups, share, width, n_tok, span, voc_cols, nz, bits, split)
    vmem = pl.BlockSpec(memory_space=pltpu.VMEM)
    anywhere = pl.BlockSpec(memory_space=pl.ANY)
    embed, capped, stats = pl.pallas_call(
        functools.partial(kernel, sizes),
        out_shape=(
            jax.ShapeDtypeStruct((share, n_tok), bf16),
            jax.ShapeDtypeStruct((n_tok, voc_cols), f32),
            jax.ShapeDtypeStruct((2, 8, n_tok), f32),
        ),
        in_specs=[anywhere, anywhere, vmem, vmem],
        out_specs=(vmem, vmem, vmem),
        scratch_shapes=[
            pltpu.VMEM((share, span), bf16),
            pltpu.VMEM((half, share, voc_cols), bf16),
            pltpu.VMEM((share, n_tok), bf16),
            pltpu.VMEM((share, n_tok), bf16),
            pltpu.VMEM((share,), bf16),
            pltpu.VMEM((n_tok, share), bf16),
            pltpu.VMEM((n_tok, share), bf16),
            pltpu.VMEM((half - 1, split, voc_cols), bf16),
            pltpu.VMEM((half - 1, split, voc_cols), bf16),
            pltpu.VMEM((half - 1, n_tok - split, voc_cols), bf16),
            pltpu.VMEM((half - 1, n_tok - split, voc_cols), bf16),
            pltpu.VMEM((share, n_tok), bf16),
            pltpu.VMEM((groups - 1, share, n_tok), bf16),
            pltpu.VMEM((share, n_tok), f32),
            pltpu.VMEM((2, 8, n_tok), f32),
            pltpu.VMEM((nz + 2, 8, n_tok), f32),
            pltpu.VMEM((2, 2, 8, n_tok), f32),
            pltpu.VMEM((nz - 1 + near, 2, 8, n_tok), f32),
            pltpu.SemaphoreType.DMA((2,)),
            pltpu.SemaphoreType.DMA((n_copies,)),
            pltpu.SemaphoreType.DMA((n_copies,)),
        ],
        compiler_params=pltpu.CompilerParams(
            collective_id=0, has_side_effects=True, vmem_limit_bytes=60 * 1024 * 1024
        ),
    )(table, hidden.T, gain, ids)
    next_embed, logprobs, chosen = pl.pallas_call(
        finish,
        out_shape=(
            jax.ShapeDtypeStruct((share, n_tok), bf16),
            jax.ShapeDtypeStruct((n_tok, voc_cols), f32),
            jax.ShapeDtypeStruct((1, n_tok), f32),
        ),
        in_specs=[vmem] * 3,
        out_specs=(vmem,) * 3,
    )(embed, capped, stats)
    return (next_embed.T, logprobs, chosen[0])


def solution(mesh):
    placed = (P("vocab", "group"), P(None, "vocab"), P("vocab"), P())
    return jax.shard_map(
        body,
        mesh=mesh,
        in_specs=placed,
        out_specs=(P(None, "vocab"), P(None, ("group", "vocab")), P()),
        check_vma=False,
    )
```

time: 229 us -> 62 us (0.27)
  waiting for transfers between devices: 90.4 us -> 0 us
  blocking collectives: 87.4 us -> 0 us
  Pallas kernels: 0 us -> 61.1 us
  local copies, waits for them, and re-layouts: 15.8 us -> 0 us
  between operations: 15.6 us -> 0.64 us
  other arithmetic: 9.93 us -> 0 us
  matrix products: 5.62 us -> 0 us
  starting transfers between devices: 3.98 us -> 0 us
    all_to_all x1 -> x0, waiting for transfers between devices: 90.3 us -> none  [body(): lax.all_to_all(table, 'vocab', split_axis=1, concat_axis=0, tiled=True)]
    psum x2 -> x0, blocking collectives: 87.4 us -> none  [the longest x1 52.4 us: body(): lax.psum((jnp.sum(jnp.exp(capped), axis=1), pick), ('group', 'vocab'))]
    pallas_call x0 -> x2, Pallas kernels: none -> 61.1 us  [the longest x1 58.8 us: body(): pl.pallas_call(functools.partial(kernel, sizes), out_shape=(jax.ShapeDtyp...]
    unnamed x8 -> x0, local copies, waits for them, and re-layouts: 8.27 us -> none
    dot_general x1 -> x0, matrix products: 5.62 us -> none  [body(): logits = jnp.dot(normed, full_cols, preferred_element_type=jnp.float32)]
    convert_element_type x4 -> x0, other arithmetic: 5.51 us -> none  [the longest x1 1.9 us: body(): found.astype(jnp.bfloat16)]
    gather x1 -> x0, local copies, waits for them, and re-layouts: 5.37 us -> none  [body(): jnp.take(table, jnp.clip(local_ids, 0, span_cols - 1), axis=1)]
    all_to_all x1 -> x0, starting transfers between devices: 3.9 us -> none  [body(): lax.all_to_all(table, 'vocab', split_axis=1, concat_axis=0, tiled=True)]
  transfers between devices with their start and end apart: 3 -> 0, of which waited for: 1 -> 0; matrix products, arithmetic and copies ran while one was open for 4% -> 0% of each run, Pallas kernels for 0% -> 0%
where the time goes in v2:
time: 62 us; the launch traced here: 61.8 us
  Pallas kernels  61.1 us (99%)
  between operations  0.64 us (1%)
    pallas_call x1, Pallas kernels, body(): pl.pallas_call(functools.partial(kernel, sizes), out_shape=(jax.ShapeDtyp...  58.8 us
    pallas_call x1, Pallas kernels, body(): pl.pallas_call(finish, out_shape=(jax.ShapeDtypeStruct((share, n_tok), bf...  2.32 us

profile of v2, /device:TPU:0, one launch (start us, length us, event | category | flops | bytes accessed | tf_op | source)
XLA Modules:
  0.0 61.8 jit_solution(688901136296710953)
XLA Ops:
  0.6 58.8 %shard_map.67 = (bf16[288,448]{1,0:T(8,128)(2,1)}, f32[448,384]{1,0:T(8,128)}, f32[2,8,448]{2,1,0:T(8,128)}) custom-call(bf16[288,6144]{1,0:T(8,128)(2,1)} %table.1, bf16[288,448]{1,0:T(8,128)(2,1)} %bitcast.3, bf16[288]{0:T(512)(128)(2,1)} %gain.1, s32[448]{0:T(512)} %ids.1), custom_call_target="tpu_custom_call" | custom-call | tf_op jit(solution)/shard_map/pallas_call | solution.py:236
  59.4 2.3 %shard_map.68 = (bf16[288,448]{1,0:T(8,128)(2,1)}, f32[448,384]{1,0:T(8,128)}, f32[1,448]{1,0:T(1,128)}) custom-call(bf16[288,448]{1,0:T(8,128)(2,1)} %get-tuple-element.9.embed, f32[448,384]{1,0:T(8,128)} %get-tuple-element.10.capped, f32[2,8,448]{2,1,0:T(8,128)} %get-tuple-element.11.stats), custom_call_target="tpu_custom_call" | custom-call | tf_op jit(solution)/shard_map/pallas_call | solution.py:272

commit v3 on v2

--- a/solution.py
+++ b/solution.py
@@ -65,8 +65,7 @@
 
     core_peer = near_peer(0, 2)
     z_peers = [z_peer(k) for k in range(1, nz)]
-    near_vocab = [near_peer(0, m) for m in range(1, 4)]
-    near_all = near_vocab + [near_peer(d, m) for d in range(1, groups) for m in range(4)]
+    near_all = [near_peer(0, m) for m in range(1, 4)] + [near_peer(d, m) for d in range(1, groups) for m in range(4)]
 
     def column(mask, core):
         return pl.ds(pl.multiple_of(place(mask, core) * voc_cols, 128), voc_cols)
@@ -89,18 +88,17 @@
     load.start()
 
     barrier = pltpu.get_barrier_semaphore()
-    everyone = z_peers + near_all
+    chip_peers = [(g, place(m, c)) for m in range(1, 2 * nz)]
+    everyone = chip_peers + [peer for m, peer in enumerate(near_all) if m != 0]
     for peer in everyone:
         pl.semaphore_signal(barrier, inc=1, device_id=peer, device_id_type=MESH)
 
     h_load.wait()
     states = hown[...].astype(f32)
-    sq = jnp.broadcast_to(jnp.sum(states * states, axis=0, keepdims=True), (8, n_tok))
-    msend[0] = sq
+    own_sq = jnp.sum(states * states, axis=0, keepdims=True)
     own_t = states.T * gain[...].astype(f32).reshape(1, share)
     pl.semaphore_wait(barrier, len(everyone))
 
-    copies = [send(msend.at[0], mrecv.at[j], peer) for j, peer in enumerate(z_peers)]
     h_copy = send(hidden, hpar, core_peer)
     g_copy = send(gain, gpar, core_peer)
     order = program_order(bits)
@@ -113,21 +111,37 @@
         t_copies[mask] = send(table.at[:, column(mask, 1 - c)], tpar.at[mask], core_peer)
 
     h_copy.wait_recv()
+    states = hpar[...].astype(f32)
+    chip_sq = own_sq + jnp.sum(states * states, axis=0, keepdims=True)
+    msend[...] = chip_sq
+    sq_copies = [send(msend, mrecv.at[j], peer) for j, peer in enumerate(chip_peers)]
+
+    def to_columns(row_list):
+        full = jnp.concatenate(row_list + [row_list[0]] * (8 - len(row_list)), axis=0)
+        full = full.T
+        return [full[:, i:i + 1] for i in range(len(row_list))]
+
+    chip_scale = to_columns([lax.rsqrt(chip_sq / width + 1e-06)])[0]
+    own_n[...] = (own_t * chip_scale).astype(bf16)
     g_copy.wait_recv()
-    par_t = hpar[...].astype(f32).T * gpar[...].astype(f32).reshape(1, share)
-
-    for j, copy in enumerate(copies):
-        copy.wait_recv()
-        sq = sq + mrecv[j]
-    msend[1] = sq
-    copies = [send(msend.at[1], mrecv.at[nz - 1 + j], peer) for j, peer in enumerate(near_vocab)]
-    for j, copy in enumerate(copies):
-        copy.wait_recv()
-        sq = sq + mrecv[nz - 1 + j]
-    scale = lax.rsqrt(sq / width + 1e-06).T[:, :1]
-    own_n[...] = (own_t * scale).astype(bf16)
-    par_n[...] = (par_t * scale).astype(bf16)
+    par_t = states.T * gpar[...].astype(f32).reshape(1, share)
+    par_n[...] = (par_t * chip_scale).astype(bf16)
     load.wait()
+
+    ratios = []
+
+    def ratio_columns():
+        if not ratios:
+            total = chip_sq
+            for j, copy in enumerate(sq_copies):
+                copy.wait_recv()
+                total = total + mrecv[j]
+            scale = lax.rsqrt(total / width + 1e-06)
+            parts = [chip_sq, mrecv[0], mrecv[1]]
+            ratios.extend(to_columns([
+                jnp.where(scale == 0.0, 0.0, scale * jnp.sqrt(part / width + 1e-06))
+                for part in parts]))
+        return ratios
 
     landed = set()
 
@@ -143,9 +157,18 @@
 
     def reduced(half, mask):
         total = partial(half, mask)
-        for bit in stage_bits(half, bits)[:stage_of(half, mask, bits)]:
+        stage = stage_of(half, mask, bits)
+        if stage == 0:
+            return total
+        low, high = rows[half]
+        own, by_y, by_z = ratio_columns()
+        total = total * own[low:high]
+        for i, bit in enumerate(stage_bits(half, bits)[:stage]):
             arrivals[half, mask | bit].wait_recv()
-            total = total + recvs[half][(mask | bit) - 1].astype(f32)
+            more = recvs[half][(mask | bit) - 1].astype(f32)
+            if i == 0:
+                more = more * (by_y if half else by_z)[low:high]
+            total = total + more
         return total
 
     chunk = 2 * voc_cols
@@ -189,31 +212,28 @@
         pick = jnp.where(spots == offsets[low:high] - first_col, capped, 0.0)
         sums.append(jnp.sum(jnp.exp(capped), axis=1, keepdims=True))
         picks.append(jnp.sum(pick, axis=1, keepdims=True))
-    sums = jnp.broadcast_to(jnp.concatenate(sums, axis=0), (n_tok, 8)).T
-    picks = jnp.broadcast_to(jnp.concatenate(picks, axis=0), (n_tok, 8)).T
+    both = [jnp.broadcast_to(jnp.concatenate(one, axis=0), (n_tok, 8)).T[:1] for one in (sums, picks)]
+    both = jnp.concatenate(both, axis=0)
     slot = 0
     for phase, peers in enumerate((z_peers, near_all)):
-        ssend[phase, 0] = sums
-        ssend[phase, 1] = picks
+        ssend[phase] = both
         copies = []
         for peer in peers:
             copies.append((slot, send(ssend.at[phase], srecv.at[slot], peer)))
             slot += 1
         for at, copy in copies:
             copy.wait_recv()
-            sums = sums + srecv[at, 0]
-            picks = picks + srecv[at, 1]
-    stats_out[0] = sums
-    stats_out[1] = picks
+            both = both + srecv[at]
+    stats_out[...] = both
     for copy in started:
         copy.wait_send()
 
 
 def finish(embed, capped, stats, embed_out, logprobs_out, chosen_out):
-    log_total = jnp.log(stats[0])
+    log_total = jnp.log(stats[0:1])
     embed_out[...] = embed[...]
-    logprobs_out[...] = capped[...] - log_total.T[:, :1]
-    chosen_out[...] = (stats[1] - log_total)[:1]
+    logprobs_out[...] = capped[...] - jnp.broadcast_to(log_total, (8, log_total.shape[1])).T[:, :1]
+    chosen_out[...] = stats[1:2] - log_total
 
 
 def body(table, hidden, gain, ids):
@@ -228,17 +248,17 @@
     bits = half.bit_length() - 1
     split = n_tok // 64 * 16
     near = 3 + 4 * (groups - 1)
-    n_copies = (nz - 1) + 3 + 2 + half + 2 * (half - 1) + (groups - 1) + (nz - 1) + near
+    n_copies = 2 + half + 3 * (half - 1) + (groups - 1) + (nz - 1) + near
     bf16, f32 = jnp.bfloat16, jnp.float32
     sizes = (groups, share, width, n_tok, span, voc_cols, nz, bits, split)
     vmem = pl.BlockSpec(memory_space=pltpu.VMEM)
-    anywhere = pl.BlockSpec(memory_space=pl.ANY)
+    anywhere = pl.BlockSpec(memory_space=pltpu.HBM)
     embed, capped, stats = pl.pallas_call(
         functools.partial(kernel, sizes),
         out_shape=(
             jax.ShapeDtypeStruct((share, n_tok), bf16),
             jax.ShapeDtypeStruct((n_tok, voc_cols), f32),
-            jax.ShapeDtypeStruct((2, 8, n_tok), f32),
+            jax.ShapeDtypeStruct((2, n_tok), f32),
         ),
         in_specs=[anywhere, anywhere, vmem, vmem],
         out_specs=(vmem, vmem, vmem),
@@ -257,10 +277,10 @@
             pltpu.VMEM((share, n_tok), bf16),
             pltpu.VMEM((groups - 1, share, n_tok), bf16),
             pltpu.VMEM((share, n_tok), f32),
-            pltpu.VMEM((2, 8, n_tok), f32),
-            pltpu.VMEM((nz + 2, 8, n_tok), f32),
-            pltpu.VMEM((2, 2, 8, n_tok), f32),
-            pltpu.VMEM((nz - 1 + near, 2, 8, n_tok), f32),
+            pltpu.VMEM((1, n_tok), f32),
+            pltpu.VMEM((half - 1, 1, n_tok), f32),
+            pltpu.VMEM((2, 2, n_tok), f32),
+            pltpu.VMEM((nz - 1 + near, 2, n_tok), f32),
             pltpu.SemaphoreType.DMA((2,)),
             pltpu.SemaphoreType.DMA((n_copies,)),
             pltpu.SemaphoreType.DMA((n_copies,)),

time: 62 us -> 58.9 us (0.950)
  Pallas kernels: 61.1 us -> 58.1 us
    pallas_call x1, Pallas kernels: 58.8 us -> 55.8 us  [body(): pl.pallas_call(functools.partial(kernel, sizes), out_shape=(jax.ShapeDtyp...]
where the time goes in v3:
time: 58.9 us; the launch traced here: 58.8 us
  Pallas kernels  58.1 us (99%)
  between operations  0.64 us (1%)
    pallas_call x1, Pallas kernels, body(): pl.pallas_call(functools.partial(kernel, sizes), out_shape=(jax.ShapeDtyp...  55.8 us
    pallas_call x1, Pallas kernels, body(): pl.pallas_call(finish, out_shape=(jax.ShapeDtypeStruct((share, n_tok), bf...  2.33 us

profile of v3, /device:TPU:0, one launch (start us, length us, event | category | flops | bytes accessed | tf_op | source)
XLA Modules:
  0.0 58.8 jit_solution(7873658949306288052)
XLA Ops:
  0.6 55.8 %shard_map.67 = (bf16[288,448]{1,0:T(8,128)(2,1)}, f32[448,384]{1,0:T(8,128)}, f32[2,448]{1,0:T(2,128)}) custom-call(bf16[288,6144]{1,0:T(8,128)(2,1)} %table.1, bf16[288,448]{1,0:T(8,128)(2,1)} %bitcast.3, bf16[288]{0:T(512)(128)(2,1)} %gain.1, s32[448]{0:T(512)} %ids.1), custom_call_target="tpu_custom_call" | custom-call | tf_op jit(solution)/shard_map/pallas_call | solution.py:256
  56.4 2.3 %shard_map.68 = (bf16[288,448]{1,0:T(8,128)(2,1)}, f32[448,384]{1,0:T(8,128)}, f32[1,448]{1,0:T(1,128)}) custom-call(bf16[288,448]{1,0:T(8,128)(2,1)} %get-tuple-element.9.embed, f32[448,384]{1,0:T(8,128)} %get-tuple-element.10.capped, f32[2,448]{1,0:T(2,128)} %get-tuple-element.11.stats), custom_call_target="tpu_custom_call" | custom-call | tf_op jit(solution)/shard_map/pallas_call | solution.py:292

commit v4 on v3

--- a/solution.py
+++ b/solution.py
@@ -27,8 +27,8 @@
 
 def program_order(bits):
     if bits == 3:
-        return [(1, 7), (0, 7), (0, 6), (1, 5), (0, 3), (0, 2), (0, 5), (1, 3), (0, 1), (1, 1),
-                None, (1, 6), (1, 4), (0, 4), (1, 2)]
+        return [(1, 7), (0, 7), (0, 6), (1, 5), (0, 3), (0, 2), (0, 5), (1, 3), (1, 6), (0, 1), (1, 1),
+                None, (1, 4), (0, 4), (1, 2)]
     every = [(half, mask) for mask in range((1 << bits) - 1, 0, -1) for half in (1, 0)]
     every.sort(key=lambda one: stage_of(one[0], one[1], bits))
     return every + [None]
@@ -286,7 +286,7 @@
             pltpu.SemaphoreType.DMA((n_copies,)),
         ],
         compiler_params=pltpu.CompilerParams(
-            collective_id=0, has_side_effects=True, vmem_limit_bytes=60 * 1024 * 1024
+            collective_id=0, has_side_effects=True, vmem_limit_bytes=52 * 1024 * 1024
         ),
     )(table, hidden.T, gain, ids)
     next_embed, logprobs, chosen = pl.pallas_call(
@@ -298,6 +298,7 @@
         ),
         in_specs=[vmem] * 3,
         out_specs=(vmem,) * 3,
+        compiler_params=pltpu.CompilerParams(vmem_limit_bytes=8 * 1024 * 1024),
     )(embed, capped, stats)
     return (next_embed.T, logprobs, chosen[0])
 

time: 58.9 us -> 56.1 us (0.952)
  Pallas kernels: 58.1 us -> 53 us
  local copies, waits for them, and re-layouts: 0 us -> 2.31 us
    pallas_call x1, Pallas kernels: 55.8 us -> 51.8 us  [body(): pl.pallas_call(functools.partial(kernel, sizes), out_shape=(jax.ShapeDtyp...]
    unnamed x0 -> x6, local copies, waits for them, and re-layouts: none -> 2.31 us
    pallas_call x1, Pallas kernels: 2.33 us -> 1.15 us  [body(): pl.pallas_call(finish, out_shape=(jax.ShapeDtypeStruct((share, n_tok), bf...]
where the time goes in v4:
time: 56.1 us; the launch traced here: 55.9 us
  Pallas kernels  53 us (94%)
  local copies, waits for them, and re-layouts  2.31 us (4%)
  between operations  0.65 us (1%)
    pallas_call x1, Pallas kernels, body(): pl.pallas_call(functools.partial(kernel, sizes), out_shape=(jax.ShapeDtyp...  51.8 us
    unnamed x6, local copies, waits for them, and re-layouts  2.31 us
    pallas_call x1, Pallas kernels, body(): pl.pallas_call(finish, out_shape=(jax.ShapeDtypeStruct((share, n_tok), bf...  1.15 us

profile of v4, /device:TPU:0, one launch (start us, length us, event | category | flops | bytes accessed | tf_op | source)
XLA Modules:
  0.0 55.9 jit_solution(2545452881662861293)
XLA Ops:
  0.6 0.0 copy-start
  0.6 1.0 %copy-done = bf16[448,288]{0,1:T(8,128)(2,1)S(1)} copy-done((bf16[448,288]{0,1:T(8,128)(2,1)S(1)}, bf16[448,288]{0,1:T(8,128)(2,1)}, u32[]{:S(2)}) %copy-start) | copy-done | bytes 258072
  1.6 0.0 copy-start.1
  1.6 0.7 %copy-done.1 = s32[448]{0:T(512)S(1)} copy-done((s32[448]{0:T(512)S(1)}, s32[448]{0:T(512)}, u32[]{:S(2)}) %copy-start.1) | copy-done | bytes 1816
  2.3 0.0 copy-start.2
  2.3 0.7 %copy-done.2 = bf16[288]{0:T(512)(128)(2,1)S(1)} copy-done((bf16[288]{0:T(512)(128)(2,1)S(1)}, bf16[288]{0:T(512)(128)(2,1)}, u32[]{:S(2)}) %copy-start.2) | copy-done | bytes 600
  3.0 51.8 %shard_map.67 = (bf16[288,448]{1,0:T(8,128)(2,1)S(1)}, f32[448,384]{1,0:T(8,128)S(1)}, f32[2,448]{1,0:T(2,128)S(1)}) custom-call(bf16[288,6144]{1,0:T(8,128)(2,1)} %table.1, bf16[288,448]{1,0:T(8,128)(2,1)S(1)} %bitcast.3, bf16[288]{0:T(512)(128)(2,1)S(1)} %copy-done.2, s32[448]{0:T(512)S(1)} %copy-done.1), custom_call_target="tpu_custom_call" | custom-call | tf_op jit(solution)/shard_map/pallas_call | solution.py:256
  54.8 1.2 %shard_map.68 = (bf16[288,448]{1,0:T(8,128)(2,1)}, f32[448,384]{1,0:T(8,128)}, f32[1,448]{1,0:T(1,128)}) custom-call(bf16[288,448]{1,0:T(8,128)(2,1)S(1)} %get-tuple-element.9.embed, f32[448,384]{1,0:T(8,128)S(1)} %get-tuple-element.10.capped, f32[2,448]{1,0:T(2,128)S(1)} %get-tuple-element.11.stats), custom_call_target="tpu_custom_call" | custom-call | tf_op jit(solution)/shard_map/pallas_call | solution.py:292
Async XLA Ops:
  0.6 1.0 %copy-start = (bf16[448,288]{0,1:T(8,128)(2,1)S(1)}, bf16[448,288]{0,1:T(8,128)(2,1)}, u32[]{:S(2)}) copy-start(bf16[448,288]{0,1:T(8,128)(2,1)} %param.5) | copy-start | bytes 774148
  1.6 0.7 %copy-start.1 = (s32[448]{0:T(512)S(1)}, s32[448]{0:T(512)}, u32[]{:S(2)}) copy-start(s32[448]{0:T(512)} %ids.1) | copy-start | bytes 5380
  2.3 0.7 %copy-start.2 = (bf16[288]{0:T(512)(128)(2,1)S(1)}, bf16[288]{0:T(512)(128)(2,1)}, u32[]{:S(2)}) copy-start(bf16[288]{0:T(512)(128)(2,1)} %gain.1) | copy-start | bytes 1732

commit v5 on v4

--- a/solution.py
+++ b/solution.py
@@ -27,8 +27,8 @@
 
 def program_order(bits):
     if bits == 3:
-        return [(1, 7), (0, 7), (0, 6), (1, 5), (0, 3), (0, 2), (0, 5), (1, 3), (1, 6), (0, 1), (1, 1),
-                None, (1, 4), (0, 4), (1, 2)]
+        return [(0, 7), (1, 7), (0, 6), (1, 5), (0, 3), (0, 2), (0, 5), (1, 3), (1, 6), (0, 1), (1, 1),
+                None, (0, 4), (1, 4), (1, 2)]
     every = [(half, mask) for mask in range((1 << bits) - 1, 0, -1) for half in (1, 0)]
     every.sort(key=lambda one: stage_of(one[0], one[1], bits))
     return every + [None]
@@ -246,7 +246,7 @@
     nz = vocab_n // 4
     half = vocab_n // 2
     bits = half.bit_length() - 1
-    split = n_tok // 64 * 16
+    split = n_tok // 112 * 32
     near = 3 + 4 * (groups - 1)
     n_copies = 2 + half + 3 * (half - 1) + (groups - 1) + (nz - 1) + near
     bf16, f32 = jnp.bfloat16, jnp.float32

time: 56.1 us -> 54.6 us (0.973)
  Pallas kernels: 53 us -> 51.4 us
    pallas_call x1, Pallas kernels: 51.8 us -> 50.3 us  [body(): pl.pallas_call(functools.partial(kernel, sizes), out_shape=(jax.ShapeDtyp...]
where the time goes in v5:
time: 54.6 us; the launch traced here: 54.4 us
  Pallas kernels  51.4 us (94%)
  local copies, waits for them, and re-layouts  2.31 us (4%)
  between operations  0.65 us (1%)
    pallas_call x1, Pallas kernels, body(): pl.pallas_call(functools.partial(kernel, sizes), out_shape=(jax.ShapeDtyp...  50.3 us
    unnamed x6, local copies, waits for them, and re-layouts  2.31 us
    pallas_call x1, Pallas kernels, body(): pl.pallas_call(finish, out_shape=(jax.ShapeDtypeStruct((share, n_tok), bf...  1.15 us

profile of v5, /device:TPU:0, one launch (start us, length us, event | category | flops | bytes accessed | tf_op | source)
XLA Modules:
  0.0 54.4 jit_solution(11307010143636661319)
XLA Ops:
  0.6 0.0 copy-start
  0.6 1.0 %copy-done = bf16[448,288]{0,1:T(8,128)(2,1)S(1)} copy-done((bf16[448,288]{0,1:T(8,128)(2,1)S(1)}, bf16[448,288]{0,1:T(8,128)(2,1)}, u32[]{:S(2)}) %copy-start) | copy-done | bytes 258072
  1.6 0.0 copy-start.1
  1.6 0.7 %copy-done.1 = s32[448]{0:T(512)S(1)} copy-done((s32[448]{0:T(512)S(1)}, s32[448]{0:T(512)}, u32[]{:S(2)}) %copy-start.1) | copy-done | bytes 1816
  2.3 0.0 copy-start.2
  2.3 0.7 %copy-done.2 = bf16[288]{0:T(512)(128)(2,1)S(1)} copy-done((bf16[288]{0:T(512)(128)(2,1)S(1)}, bf16[288]{0:T(512)(128)(2,1)}, u32[]{:S(2)}) %copy-start.2) | copy-done | bytes 600
  3.0 50.3 %shard_map.67 = (bf16[288,448]{1,0:T(8,128)(2,1)S(1)}, f32[448,384]{1,0:T(8,128)S(1)}, f32[2,448]{1,0:T(2,128)S(1)}) custom-call(bf16[288,6144]{1,0:T(8,128)(2,1)} %table.1, bf16[288,448]{1,0:T(8,128)(2,1)S(1)} %bitcast.3, bf16[288]{0:T(512)(128)(2,1)S(1)} %copy-done.2, s32[448]{0:T(512)S(1)} %copy-done.1), custom_call_target="tpu_custom_call" | custom-call | tf_op jit(solution)/shard_map/pallas_call | solution.py:256
  53.2 1.2 %shard_map.68 = (bf16[288,448]{1,0:T(8,128)(2,1)}, f32[448,384]{1,0:T(8,128)}, f32[1,448]{1,0:T(1,128)}) custom-call(bf16[288,448]{1,0:T(8,128)(2,1)S(1)} %get-tuple-element.9.embed, f32[448,384]{1,0:T(8,128)S(1)} %get-tuple-element.10.capped, f32[2,448]{1,0:T(2,128)S(1)} %get-tuple-element.11.stats), custom_call_target="tpu_custom_call" | custom-call | tf_op jit(solution)/shard_map/pallas_call | solution.py:292
Async XLA Ops:
  0.6 1.0 %copy-start = (bf16[448,288]{0,1:T(8,128)(2,1)S(1)}, bf16[448,288]{0,1:T(8,128)(2,1)}, u32[]{:S(2)}) copy-start(bf16[448,288]{0,1:T(8,128)(2,1)} %param.5) | copy-start | bytes 774148
  1.6 0.7 %copy-start.1 = (s32[448]{0:T(512)S(1)}, s32[448]{0:T(512)}, u32[]{:S(2)}) copy-start(s32[448]{0:T(512)} %ids.1) | copy-start | bytes 5380
  2.3 0.7 %copy-start.2 = (bf16[288]{0:T(512)(128)(2,1)S(1)}, bf16[288]{0:T(512)(128)(2,1)}, u32[]{:S(2)}) copy-start(bf16[288]{0:T(512)(128)(2,1)} %gain.1) | copy-start | bytes 1732
